TPU v7x, 32 devices: a whole 2x2x4 slice. The times are simulated.
32 devices in a mesh: shard: 4 (over z), tensor: 4 (over x, core), section: 2 (over y).
Axes of the slice: x: 2, y: 2, z: 4, core: 2. Of those that a mesh axis runs over, the one named last changes fastest.
Arguments:
- hidden_acts: bfloat16 [2, 10240, 4096], P('section', 'shard', 'tensor'), may hold values from -8 to 8
- out_grads: bfloat16 [2, 10240, 1024], P('section', 'shard'), may hold values from -8 to 8
- errors: float32 [2, 4, 1024, 4096], P('section', 'shard', None, 'tensor'), may hold values from -3 to 3
- factors: float32 [2, 32, 4096], P('section', None, 'tensor'), may hold values from -6 to 6
- whiten: float32 [2, 2, 32, 32], P('section'), may hold values from -1.5 to 3
- momentum: float32 [2, 1024, 4096], P('section', 'shard', 'tensor'), may hold values from -3 to 3
- master: float32 [2, 1024, 4096], P('section', 'shard', 'tensor'), may hold values from -3 to 3
- table: bfloat16 [32768, 1024], P(('shard', 'section'), 'tensor'), may hold values from -5 to 5
- touched_ids: int32 [1024], P(('shard', 'section')), may hold values from 0 to 32767, as said below
- touched_grads: bfloat16 [1024, 1024], P(('shard', 'section'), 'tensor'), may hold values from -5 to 5
Outputs:
- new_errors: float32 [2, 4, 1024, 4096], P('section', 'shard', None, 'tensor')
- new_factors: float32 [2, 32, 4096], P('section', None, 'tensor')
- new_momentum: float32 [2, 1024, 4096], P('section', 'shard', 'tensor')
- new_master: float32 [2, 1024, 4096], P('section', 'shard', 'tensor')
- new_weights: bfloat16 [2, 1024, 4096], P('section', None, 'tensor')
- new_table: bfloat16 [32768, 1024], P(('shard', 'section'), 'tensor')
Inputs may be any that keep to these rules, and one draw needn't show every extreme that they name: `touched_ids`: the 128 ids of one device of shard and section name at most 32 rows in each block of 4096 vocabulary rows; in every draw one block receives exactly 32 rows from every device.
All inputs are finite; a program needn't handle non-finite values.
Results may differ from a plain program's by a relative error of at most 0.0036.
Values may be sent and summed in bfloat16 or wider, within the bound.
A program may use at most 128 MiB of HBM per device.

v0:
```python
import jax
import jax.numpy as jnp
from jax import lax
from jax.sharding import PartitionSpec as P

D = 1024
FF = 4096
ROUNDS = 2
epsilon = 1e-06
momentum_decay = 0.9
learn_rate = 0.1
embed_rate = 0.25
clip_level = 0.03
highest = lax.Precision.HIGHEST


def on_device(
    hidden_acts,
    out_grads,
    errors,
    factors,
    whiten,
    momentum,
    master,
    table,
    touched_ids,
    touched_grads,
):
    shards = lax.axis_size("shard")
    grad_block = lax.dot_general(
        out_grads[0], hidden_acts[0], (((0,), (0,)), ((), ())), preferred_element_type=jnp.float32
    )
    rounded = lax.optimization_barrier(grad_block.astype(jnp.bfloat16))
    corrected = rounded.astype(jnp.float32) + errors[0, 0]
    right_part = factors[0]
    rank_count = right_part.shape[0]
    left_unit = None
    for power_round in range(ROUNDS):
        left_part = lax.dot_general(
            right_part,
            corrected,
            (((1,), (1,)), ((), ())),
            precision=highest,
            preferred_element_type=jnp.float32,
        )
        left_sum = lax.psum(left_part, ("shard", "tensor"))
        whitened = jnp.dot(whiten[0, power_round].T, left_sum, precision=highest)
        scaling = lax.rsqrt(jnp.sum(whitened * whitened) / rank_count + epsilon)
        left_unit = whitened * scaling
        right_local = jnp.dot(left_unit, corrected, precision=highest)
        right_part = lax.psum(right_local, "shard") / shards
    gram_left = jnp.dot(left_unit, left_unit.T, precision=highest)
    gram_right = jnp.dot(right_part, right_part.T, precision=highest)
    total_squares = lax.psum(jnp.sum(gram_left * gram_right), ("tensor", "section"))
    approx = lax.dot_general(
        left_unit,
        right_part,
        (((0,), (0,)), ((), ())),
        precision=highest,
        preferred_element_type=jnp.float32,
    )
    new_errors = (corrected - approx)[None, None]
    entries = lax.axis_size("section") * D * FF
    spread = jnp.sqrt(total_squares / entries + epsilon)
    clip_factor = jnp.minimum(1.0, clip_level / spread)
    rows_own = momentum.shape[1]
    row_start = lax.axis_index("shard") * rows_own
    approx_rows = lax.dynamic_slice_in_dim(approx, row_start, rows_own, 0)
    new_momentum = momentum_decay * momentum + clip_factor * approx_rows[None]
    new_master = master - learn_rate * new_momentum
    new_weights = lax.all_gather(new_master.astype(jnp.bfloat16), "shard", axis=1, tiled=True)
    new_factors = right_part[None]
    vocab_rows = table.shape[0]
    table_width = table.shape[1]
    first_row = lax.axis_index(("shard", "section")) * vocab_rows
    recv_rows, recv_ids = (
        lax.all_gather(touched_grads, ("shard", "section"), axis=0, tiled=True),
        lax.all_gather(touched_ids, ("shard", "section"), axis=0, tiled=True),
    )
    local_index = recv_ids - first_row
    inside = (local_index >= 0) & (local_index < vocab_rows)
    target = jnp.where(inside, local_index, vocab_rows)
    table_grad = (
        jnp.zeros((vocab_rows, table_width), jnp.float32)
        .at[target]
        .add(recv_rows.astype(jnp.float32), mode="drop")
    )
    new_table = (table.astype(jnp.float32) - embed_rate * table_grad).astype(jnp.bfloat16)
    return (new_errors, new_factors, new_momentum, new_master, new_weights, new_table)


def solution(mesh):
    in_specs = (
        P("section", "shard", "tensor"),
        P("section", "shard", None),
        P("section", "shard", None, "tensor"),
        P("section", None, "tensor"),
        P("section", None, None, None),
        P("section", "shard", "tensor"),
        P("section", "shard", "tensor"),
        P(("shard", "section"), "tensor"),
        P(("shard", "section")),
        P(("shard", "section"), "tensor"),
    )
    out_specs = (
        P("section", "shard", None, "tensor"),
        P("section", None, "tensor"),
        P("section", "shard", "tensor"),
        P("section", "shard", "tensor"),
        P("section", None, "tensor"),
        P(("shard", "section"), "tensor"),
    )
    return jax.shard_map(
        on_device, mesh=mesh, in_specs=in_specs, out_specs=out_specs, check_vma=False
    )
```

profile of v0, /device:TPU:0, one launch (start us, length us, event | category | flops | bytes accessed | tf_op | source)
XLA Modules:
  0.0 398.0 jit_solution(17824651592674097183)
XLA Ops:
  7.2 9.3 %fusion.5 = bf16[1024,1024]{1,0:T(8,128)(2,1)S(1)} fusion(bf16[1,2560,1024]{2,1,0:T(8,128)(2,1)} %param.10, bf16[1,2560,1024]{2,1,0:T(8,128)(2,1)} %param.11), kind=kOutput, calls=%fused_computation.9 | convolution fusion | flops 5369757696 | bytes 12582912 | tf_op jit(solution)/shard_map/dot_general | solution.py:30
  16.6 4.7 %convolution_bitcast_fusion = f32[32,1024]{1,0:T(8,128)} fusion(f32[1,32,1024]{2,1,0:T(8,128)S(1)} %copy-done, f32[1,1,1024,1024]{3,2,1,0:T(8,128)S(1)} %copy-done.1, bf16[1024,1024]{1,0:T(8,128)(2,1)S(1)} %fusion.5), kind=kOutput, calls=%fused_computation.10 | convolution fusion | flops 404750336 | bytes 6553600 | tf_op jit(solution)/shard_map/dot_general | solution.py:39
  21.3 89.8 %all-reduce.5.cloned.1.call-done = f32[32,1024]{1,0:T(8,128)} async-done(((f32[32,1024]{1,0:T(8,128)}), f32[32,1024]{1,0:T(8,128)}) %all-reduce.5.cloned.1.call-update) | async-done | bytes 131088 | tf_op jit(solution)/shard_map/psum | solution.py:46
  111.1 1.8 multiply_reduce_fusion.1
  113.7 5.6 %fusion.15 = f32[32,1024]{1,0:T(8,128)} fusion(f32[1024,32]{0,1:T(8,128)S(1)} %get-tuple-element.10, f32[]{:T(128)S(6)} %rsqrt.7, f32[1,1,1024,1024]{3,2,1,0:T(8,128)} %param.12, bf16[1024,1024]{1,0:T(8,128)(2,1)S(1)} %fusion.5), kind=kOutput, calls=%fused_computation.20 | convolution fusion | flops 404783104 | bytes 6553604 | tf_op jit(solution)/shard_map/dot_general | solution.py:50
  119.3 36.2 %all-reduce.7.cloned.1.call-done = f32[32,1024]{1,0:T(8,128)} async-done(((f32[32,1024]{1,0:T(8,128)}), f32[32,1024]{1,0:T(8,128)}) %all-reduce.7.cloned.1.call-update) | async-done | bytes 131088 | tf_op jit(solution)/shard_map/psum | solution.py:51
  155.5 6.8 %fusion.13 = f32[32,1024]{1,0:T(8,128)} fusion(f32[32,1024]{1,0:T(8,128)} %all-reduce.7.cloned.1.call-done, f32[1,1,1024,1024]{3,2,1,0:T(8,128)} %param.12, bf16[1024,1024]{1,0:T(8,128)(2,1)S(1)} %fusion.5), kind=kOutput, calls=%fused_computation.18 | convolution fusion | flops 404783104 | bytes 6553600 | tf_op jit(solution)/shard_map/dot_general | solution.py:39
  162.5 86.6 %all-reduce.9.cloned.1.call-done = f32[32,1024]{1,0:T(8,128)} async-done(((f32[32,1024]{1,0:T(8,128)}), f32[32,1024]{1,0:T(8,128)}) %all-reduce.9.cloned.1.call-update) | async-done | bytes 131088 | tf_op jit(solution)/shard_map/psum | solution.py:46
  249.1 1.8 multiply_reduce_fusion
  251.6 5.6 %fusion.23 = f32[32,1024]{1,0:T(8,128)} fusion(f32[1024,32]{0,1:T(8,128)S(1)} %get-tuple-element.12, f32[]{:T(128)S(6)} %rsqrt.8, f32[1,1,1024,1024]{3,2,1,0:T(8,128)} %param.12, bf16[1024,1024]{1,0:T(8,128)(2,1)S(1)} %fusion.5), kind=kOutput, calls=%fused_computation.30 | convolution fusion | flops 404783104 | bytes 6553604 | tf_op jit(solution)/shard_map/dot_general | solution.py:50
  257.6 36.0 %all-reduce.11.cloned.1.call-done = f32[32,1024]{1,0:T(8,128)} async-done(((f32[32,1024]{1,0:T(8,128)}), f32[32,1024]{1,0:T(8,128)}) %all-reduce.11.cloned.1.call-update) | async-done | bytes 131088 | tf_op jit(solution)/shard_map/psum | solution.py:51
  293.6 1.8 fusion.11
  295.4 14.0 %psum.39 = f32[]{:T(128)} all-reduce(f32[]{:T(128)} %fusion.11), channel_id=1, replica_groups=mesh['shard'=4,'tensor'=4,'section'=2] {'tensor','section'}, use_global_device_ids=true, to_apply=%region_7.0 | all-reduce | flops 1 | bytes 8 | tf_op jit(solution)/shard_map/psum | solution.py:54
  310.1 4.5 %fusion.18 = f32[1024,1024]{1,0:T(8,128)S(1)} fusion(f32[32,1024]{1,0:T(8,128)} %all-reduce.11.cloned.1.call-done, f32[1024,32]{0,1:T(8,128)S(1)} %get-tuple-element.12, f32[]{:T(128)S(6)} %rsqrt.8), kind=kOutput, calls=%fused_computation.25 | convolution fusion | flops 402718720 | bytes 4456452 | tf_op jit(solution)/shard_map/dot_general | solution.py:55
  314.6 2.0 copy-done.3
  316.6 1.9 fusion.41
  318.6 18.6 %all-gather = s32[8,1,128]{2,1,0:T(1,128)S(1)} all-gather(s32[1,1,128]{2,1,0:T(1,128)S(1)} %bitcast.48), channel_id=1, replica_groups=mesh['shard'=4,'tensor'=4,'section'=2] {'shard','section'}, dimensions={0}, use_global_device_ids=true | all-gather | bytes 4608 | tf_op jit(solution)/shard_map/all_gather | solution.py:78
  337.2 33.2 %all_gather.11 = bf16[1024,256]{1,0:T(8,128)(2,1)S(1)} all-gather(bf16[128,256]{1,0:T(8,128)(2,1)S(1)} %copy-done.8), channel_id=1, replica_groups=mesh['shard'=4,'tensor'=4,'section'=2] {'shard','section'}, dimensions={0}, use_global_device_ids=true | all-gather | bytes 589824 | tf_op jit(solution)/shard_map/all_gather | solution.py:77
  370.3 8.3 %scatter_custom_fusion = f32[4096,256]{1,0:T(8,128)} fusion(s32[1024]{0:T(1024)S(1)} %compare_select_fusion, f32[]{:T(128)} %constant.16.clone.1, bf16[1024,256]{1,0:T(8,128)(2,1)S(1)} %all_gather.11), kind=kCustom, calls=%fused_computation.7 | custom fusion | flops 524288 | bytes 4718596 | tf_op jit(solution)/shard_map/scatter-add | solution.py:86
  378.6 4.8 %subtract_convert_fusion = bf16[4096,256]{1,0:T(8,128)(2,1)} fusion(f32[4096,256]{1,0:T(8,128)} %scatter_custom_fusion, bf16[4096,256]{1,0:T(8,128)(2,1)} %param.17), kind=kLoop, calls=%fused_computation.5 | loop fusion | flops 4194304 | bytes 8388608 | tf_op jit(solution)/shard_map/convert_element_type | solution.py:88
  383.4 0.7 multiply_bitcast_fusion
  384.1 0.6 copy-done.4
  384.7 3.6 subtract_bitcast_fusion
  388.3 3.1 copy.21
  (34 shorter events, 0.8 us)
Async XLA Ops:
  7.2 9.4 %copy-start = (f32[1,32,1024]{2,1,0:T(8,128)S(1)}, f32[1,32,1024]{2,1,0:T(8,128)}, u32[]{:S(2)}) copy-start(f32[1,32,1024]{2,1,0:T(8,128)} %param.13) | copy-start | bytes 393220
  7.2 103.9 %all-reduce.5.cloned.1.call-start = ((), (), s32[]{:S(2)}) async-start(), calls=%async_computation | async-start | bytes 262144 | tf_op jit(solution)/shard_map/psum | solution.py:46
  7.2 9.3 %copy-start.1 = (f32[1,1,1024,1024]{3,2,1,0:T(8,128)S(1)}, f32[1,1,1024,1024]{3,2,1,0:T(8,128)}, u32[]{:S(2)}) copy-start(f32[1,1,1024,1024]{3,2,1,0:T(8,128)} %param.12) | copy-start | bytes 12582916
  16.5 94.6 %copy-start.9 = (f32[1,2,32,32]{3,2,1,0:T(8,128)S(1)}, f32[1,2,32,32]{3,2,1,0:T(8,128)}, u32[]{:S(2)}) copy-start(f32[1,2,32,32]{3,2,1,0:T(8,128)} %param.14) | copy-start | bytes 24580
  21.3 134.2 %all-reduce.7.cloned.1.call-start = ((), (), s32[]{:S(2)}) async-start(), calls=%async_computation.1 | async-start | bytes 262144 | tf_op jit(solution)/shard_map/psum | solution.py:51
  119.2 129.8 %all-reduce.9.cloned.1.call-start = ((), (), s32[]{:S(2)}) async-start(), calls=%async_computation.2 | async-start | bytes 262144 | tf_op jit(solution)/shard_map/psum | solution.py:46
  162.3 131.3 %all-reduce.11.cloned.1.call-start = ((), (), s32[]{:S(2)}) async-start(), calls=%async_computation.3 | async-start | bytes 262144 | tf_op jit(solution)/shard_map/psum | solution.py:51
  251.6 65.0 %copy-start.6 = (f32[1,256,1024]{2,1,0:T(8,128)S(1)}, f32[1,256,1024]{2,1,0:T(8,128)}, u32[]{:S(2)}) copy-start(f32[1,256,1024]{2,1,0:T(8,128)} %param.16) | copy-start | bytes 3145732
  257.3 131.1 %all-gather.3.cloned.1.call-start = ((), (), s32[]{:S(2)}) async-start(), calls=%async_computation.4 | async-start | bytes 2621440 | tf_op jit(solution)/shard_map/all_gather | solution.py:71
  310.1 6.5 %copy-start.7 = (f32[1,256,1024]{2,1,0:T(8,128)S(1)}, f32[1,256,1024]{2,1,0:T(8,128)}, u32[]{:S(2)}) copy-start(f32[1,256,1024]{2,1,0:T(8,128)} %param.15) | copy-start | bytes 3145732
  314.6 2.0 copy-start.3
  316.6 2.0 copy-start.10
  316.6 20.6 %copy-start.8 = (bf16[128,256]{1,0:T(8,128)(2,1)S(1)}, bf16[128,256]{1,0:T(8,128)(2,1)}, u32[]{:S(2)}) copy-start(bf16[128,256]{1,0:T(8,128)(2,1)} %param.19) | copy-start | bytes 196612
  370.3 13.1 %copy-start.5 = (f32[32,1024]{1,0:T(8,128)S(1)}, f32[32,1024]{1,0:T(8,128)}, u32[]{:S(2)}) copy-start(f32[32,1024]{1,0:T(8,128)} %all-reduce.11.cloned.1.call-done) | copy-start | bytes 393220
  378.6 5.5 %copy-start.2 = (f32[1,1,1024,1024]{3,2,1,0:T(8,128)S(1)}, f32[1,1,1024,1024]{3,2,1,0:T(8,128)}, u32[]{:S(2)}) copy-start(f32[1,1,1024,1024]{3,2,1,0:T(8,128)} %param.12) | copy-start | bytes 12582916
  378.6 6.1 %copy-start.4 = (f32[1024,1024]{1,0:T(8,128)S(1)}, f32[1024,1024]{1,0:T(8,128)}, u32[]{:S(2)}) copy-start(f32[1024,1024]{1,0:T(8,128)} %copy-done.3) | copy-start | bytes 12582916
Sparse Core Ops, SparseCore 0:
  21.4 89.6 all-reduce.4
  119.4 36.0 all-reduce.6
  162.4 86.6 all-reduce.8
  257.4 36.1 all-reduce.10
  318.7 49.5 all-gather.2
where the time goes:
time: 398 us
  waiting for transfers between devices  249 us (63%)
  blocking collectives  65.7 us (17%)
  matrix products  42.2 us (11%)
  other arithmetic  19.3 us (5%)
  between operations  16 us (4%)
  local copies, waits for them, and re-layouts  5.77 us (1%)
    psum x2, waiting for transfers between devices, on_device(): left_sum = lax.psum(left_part, ('shard', 'tensor'))  176 us
    psum x2, waiting for transfers between devices, on_device(): right_part = lax.psum(right_local, 'shard') / shards  72.2 us
    all_gather x1, blocking collectives, on_device(): lax.all_gather(touched_grads, ('shard', 'section'), axis=0, tiled=True)  33.2 us
    all_gather x1, blocking collectives, on_device(): lax.all_gather(touched_ids, ('shard', 'section'), axis=0, tiled=True)  18.6 us
    psum x1, blocking collectives, on_device(): lax.psum(jnp.sum(gram_left * gram_right), ('tensor', 'section'))  14 us
    dot_general x2, matrix products, on_device(): lax.dot_general(right_part, corrected, (((1,), (1,)), ((), ())), precisio...  11.4 us
    dot_general x2, matrix products, on_device(): right_local = jnp.dot(left_unit, corrected, precision=highest)  11.2 us
    dot_general x1, matrix products, on_device(): lax.dot_general(out_grads[0], hidden_acts[0], (((0,), (0,)), ((), ())), p...  9.28 us
  transfers between devices with their start and end apart: 5, of which 4 were waited for; matrix products, arithmetic and copies ran while one was open for 4% of the time, Pallas kernels for 0%

commit v1 on v0

--- a/solution.py
+++ b/solution.py
@@ -43,7 +43,9 @@
             precision=highest,
             preferred_element_type=jnp.float32,
         )
-        left_sum = lax.psum(left_part, ("shard", "tensor"))
+        left_sum = left_part
+        for name in ("tensor", "shard"):
+            left_sum = lax.psum(left_sum, name)
         whitened = jnp.dot(whiten[0, power_round].T, left_sum, precision=highest)
         scaling = lax.rsqrt(jnp.sum(whitened * whitened) / rank_count + epsilon)
         left_unit = whitened * scaling

time: 398 us -> 357 us (0.90)
  waiting for transfers between devices: 249 us -> 207 us
    psum x2 -> x4, waiting for transfers between devices: 176 us -> 139 us  [on_device(): left_sum = lax.psum(left_sum, name)]
    psum x2, waiting for transfers between devices: 72.2 us -> 68.1 us  [on_device(): right_part = lax.psum(right_local, 'shard') / shards]
  transfers between devices with their start and end apart: 5 -> 7, of which waited for: 4 -> 6; matrix products, arithmetic and copies ran while one was open for 4% -> 5% of each run, Pallas kernels for 0% -> 0%
where the time goes in v1:
time: 357 us; the launch traced here: 356 us
  waiting for transfers between devices  207 us (58%)
  blocking collectives  65.7 us (18%)
  matrix products  42.2 us (12%)
  other arithmetic  19.3 us (5%)
  between operations  16.3 us (5%)
  local copies, waits for them, and re-layouts  5.77 us (2%)
    psum x4, waiting for transfers between devices, on_device(): left_sum = lax.psum(left_sum, name)  139 us
    psum x2, waiting for transfers between devices, on_device(): right_part = lax.psum(right_local, 'shard') / shards  68.1 us
    all_gather x1, blocking collectives, on_device(): lax.all_gather(touched_grads, ('shard', 'section'), axis=0, tiled=True)  33.1 us
    all_gather x1, blocking collectives, on_device(): lax.all_gather(touched_ids, ('shard', 'section'), axis=0, tiled=True)  18.6 us
    psum x1, blocking collectives, on_device(): lax.psum(jnp.sum(gram_left * gram_right), ('tensor', 'section'))  14 us
    dot_general x2, matrix products, on_device(): lax.dot_general(right_part, corrected, (((1,), (1,)), ((), ())), precisio...  11.4 us
    dot_general x2, matrix products, on_device(): right_local = jnp.dot(left_unit, corrected, precision=highest)  11.2 us
    dot_general x1, matrix products, on_device(): lax.dot_general(out_grads[0], hidden_acts[0], (((0,), (0,)), ((), ())), p...  9.28 us
  transfers between devices with their start and end apart: 7, of which 6 were waited for; matrix products, arithmetic and copies ran while one was open for 5% of the time, Pallas kernels for 0%

profile of v1, /device:TPU:0, one launch (start us, length us, event | category | flops | bytes accessed | tf_op | source)
XLA Modules:
  0.0 356.5 jit_solution(6560132471694611748)
XLA Ops:
  7.2 9.3 %fusion.5 = bf16[1024,1024]{1,0:T(8,128)(2,1)S(1)} fusion(bf16[1,2560,1024]{2,1,0:T(8,128)(2,1)} %param.10, bf16[1,2560,1024]{2,1,0:T(8,128)(2,1)} %param.11), kind=kOutput, calls=%fused_computation.9 | convolution fusion | flops 5369757696 | bytes 12582912 | tf_op jit(solution)/shard_map/dot_general | solution.py:30
  16.6 4.7 %convolution_bitcast_fusion = f32[32,1024]{1,0:T(8,128)} fusion(f32[1,32,1024]{2,1,0:T(8,128)S(1)} %copy-done, f32[1,1,1024,1024]{3,2,1,0:T(8,128)S(1)} %copy-done.1, bf16[1024,1024]{1,0:T(8,128)(2,1)S(1)} %fusion.5), kind=kOutput, calls=%fused_computation.10 | convolution fusion | flops 404750336 | bytes 6553600 | tf_op jit(solution)/shard_map/dot_general | solution.py:39
  21.3 34.2 %all-reduce.7.cloned.1.call-done = f32[32,1024]{1,0:T(8,128)} async-done(((f32[32,1024]{1,0:T(8,128)}), f32[32,1024]{1,0:T(8,128)}) %all-reduce.7.cloned.1.call-update) | async-done | bytes 131088 | tf_op jit(solution)/shard_map/psum | solution.py:48
  55.6 36.8 %all-reduce.9.cloned.1.call-done = f32[32,1024]{1,0:T(8,128)} async-done(((f32[32,1024]{1,0:T(8,128)}), f32[32,1024]{1,0:T(8,128)}) %all-reduce.9.cloned.1.call-update) | async-done | bytes 131088 | tf_op jit(solution)/shard_map/psum | solution.py:48
  92.4 1.8 multiply_reduce_fusion.1
  94.9 5.6 %fusion.15 = f32[32,1024]{1,0:T(8,128)} fusion(f32[1024,32]{0,1:T(8,128)S(1)} %get-tuple-element.10, f32[]{:T(128)S(6)} %rsqrt.7, f32[1,1,1024,1024]{3,2,1,0:T(8,128)} %param.12, bf16[1024,1024]{1,0:T(8,128)(2,1)S(1)} %fusion.5), kind=kOutput, calls=%fused_computation.20 | convolution fusion | flops 404783104 | bytes 6553604 | tf_op jit(solution)/shard_map/dot_general | solution.py:52
  100.6 34.2 %all-reduce.11.cloned.1.call-done = f32[32,1024]{1,0:T(8,128)} async-done(((f32[32,1024]{1,0:T(8,128)}), f32[32,1024]{1,0:T(8,128)}) %all-reduce.11.cloned.1.call-update) | async-done | bytes 131088 | tf_op jit(solution)/shard_map/psum | solution.py:53
  134.8 6.8 %fusion.13 = f32[32,1024]{1,0:T(8,128)} fusion(f32[32,1024]{1,0:T(8,128)} %all-reduce.11.cloned.1.call-done, f32[1,1,1024,1024]{3,2,1,0:T(8,128)} %param.12, bf16[1024,1024]{1,0:T(8,128)(2,1)S(1)} %fusion.5), kind=kOutput, calls=%fused_computation.18 | convolution fusion | flops 404783104 | bytes 6553600 | tf_op jit(solution)/shard_map/dot_general | solution.py:39
  141.6 31.1 %all-reduce.13.cloned.1.call-done = f32[32,1024]{1,0:T(8,128)} async-done(((f32[32,1024]{1,0:T(8,128)}), f32[32,1024]{1,0:T(8,128)}) %all-reduce.13.cloned.1.call-update) | async-done | bytes 131088 | tf_op jit(solution)/shard_map/psum | solution.py:48
  173.0 36.4 %all-reduce.15.cloned.1.call-done = f32[32,1024]{1,0:T(8,128)} async-done(((f32[32,1024]{1,0:T(8,128)}), f32[32,1024]{1,0:T(8,128)}) %all-reduce.15.cloned.1.call-update) | async-done | bytes 131088 | tf_op jit(solution)/shard_map/psum | solution.py:48
  209.4 1.8 multiply_reduce_fusion
  211.9 5.6 %fusion.23 = f32[32,1024]{1,0:T(8,128)} fusion(f32[1024,32]{0,1:T(8,128)S(1)} %get-tuple-element.12, f32[]{:T(128)S(6)} %rsqrt.8, f32[1,1,1024,1024]{3,2,1,0:T(8,128)} %param.12, bf16[1024,1024]{1,0:T(8,128)(2,1)S(1)} %fusion.5), kind=kOutput, calls=%fused_computation.30 | convolution fusion | flops 404783104 | bytes 6553604 | tf_op jit(solution)/shard_map/dot_general | solution.py:52
  217.9 33.9 %all-reduce.17.cloned.1.call-done = f32[32,1024]{1,0:T(8,128)} async-done(((f32[32,1024]{1,0:T(8,128)}), f32[32,1024]{1,0:T(8,128)}) %all-reduce.17.cloned.1.call-update) | async-done | bytes 131088 | tf_op jit(solution)/shard_map/psum | solution.py:53
  251.9 1.8 fusion.11
  253.7 14.0 %psum.55 = f32[]{:T(128)} all-reduce(f32[]{:T(128)} %fusion.11), channel_id=1, replica_groups=mesh['shard'=4,'tensor'=4,'section'=2] {'tensor','section'}, use_global_device_ids=true, to_apply=%region_9.0 | all-reduce | flops 1 | bytes 8 | tf_op jit(solution)/shard_map/psum | solution.py:56
  268.4 4.5 %fusion.18 = f32[1024,1024]{1,0:T(8,128)S(1)} fusion(f32[32,1024]{1,0:T(8,128)} %all-reduce.17.cloned.1.call-done, f32[1024,32]{0,1:T(8,128)S(1)} %get-tuple-element.12, f32[]{:T(128)S(6)} %rsqrt.8), kind=kOutput, calls=%fused_computation.25 | convolution fusion | flops 402718720 | bytes 4456452 | tf_op jit(solution)/shard_map/dot_general | solution.py:57
  272.9 2.0 copy-done.3
  274.9 1.9 fusion.41
  276.9 18.6 %all-gather = s32[8,1,128]{2,1,0:T(1,128)S(1)} all-gather(s32[1,1,128]{2,1,0:T(1,128)S(1)} %bitcast.48), channel_id=1, replica_groups=mesh['shard'=4,'tensor'=4,'section'=2] {'shard','section'}, dimensions={0}, use_global_device_ids=true | all-gather | bytes 4608 | tf_op jit(solution)/shard_map/all_gather | solution.py:80
  295.5 33.1 %all_gather.11 = bf16[1024,256]{1,0:T(8,128)(2,1)S(1)} all-gather(bf16[128,256]{1,0:T(8,128)(2,1)S(1)} %copy-done.8), channel_id=1, replica_groups=mesh['shard'=4,'tensor'=4,'section'=2] {'shard','section'}, dimensions={0}, use_global_device_ids=true | all-gather | bytes 589824 | tf_op jit(solution)/shard_map/all_gather | solution.py:79
  328.5 8.3 %scatter_custom_fusion = f32[4096,256]{1,0:T(8,128)} fusion(s32[1024]{0:T(1024)S(1)} %compare_select_fusion, f32[]{:T(128)} %constant.16.clone.1, bf16[1024,256]{1,0:T(8,128)(2,1)S(1)} %all_gather.11), kind=kCustom, calls=%fused_computation.7 | custom fusion | flops 524288 | bytes 4718596 | tf_op jit(solution)/shard_map/scatter-add | solution.py:88
  336.8 4.8 %subtract_convert_fusion = bf16[4096,256]{1,0:T(8,128)(2,1)} fusion(f32[4096,256]{1,0:T(8,128)} %scatter_custom_fusion, bf16[4096,256]{1,0:T(8,128)(2,1)} %param.17), kind=kLoop, calls=%fused_computation.5 | loop fusion | flops 4194304 | bytes 8388608 | tf_op jit(solution)/shard_map/convert_element_type | solution.py:90
  342.9 3.6 %subtract_bitcast_fusion = f32[1,1,1024,1024]{3,2,1,0:T(8,128)} fusion(f32[1024,1024]{1,0:T(8,128)S(1)} %copy-done.4, f32[1,1,1024,1024]{3,2,1,0:T(8,128)S(1)} %copy-done.2, bf16[1024,1024]{1,0:T(8,128)(2,1)S(1)} %fusion.5), kind=kLoop, calls=%fused_computation.6 | loop fusion | flops 3145728 | bytes 14680064 | tf_op jit(solution)/shard_map/broadcast_in_dim | solution.py:64
  346.6 3.1 copy.23
  (40 shorter events, 2.2 us)
Async XLA Ops:
  7.2 9.4 %copy-start = (f32[1,32,1024]{2,1,0:T(8,128)S(1)}, f32[1,32,1024]{2,1,0:T(8,128)}, u32[]{:S(2)}) copy-start(f32[1,32,1024]{2,1,0:T(8,128)} %param.13) | copy-start | bytes 393220
  7.2 48.3 %all-reduce.7.cloned.1.call-start = ((), (), s32[]{:S(2)}) async-start(), calls=%async_computation | async-start | bytes 262144 | tf_op jit(solution)/shard_map/psum | solution.py:48
  7.2 9.3 %copy-start.1 = (f32[1,1,1024,1024]{3,2,1,0:T(8,128)S(1)}, f32[1,1,1024,1024]{3,2,1,0:T(8,128)}, u32[]{:S(2)}) copy-start(f32[1,1,1024,1024]{3,2,1,0:T(8,128)} %param.12) | copy-start | bytes 12582916
  16.5 75.9 %copy-start.9 = (f32[1,2,32,32]{3,2,1,0:T(8,128)S(1)}, f32[1,2,32,32]{3,2,1,0:T(8,128)}, u32[]{:S(2)}) copy-start(f32[1,2,32,32]{3,2,1,0:T(8,128)} %param.14) | copy-start | bytes 24580
  21.3 71.1 %all-reduce.9.cloned.1.call-start = ((), (), s32[]{:S(2)}) async-start(), calls=%async_computation.1 | async-start | bytes 262144 | tf_op jit(solution)/shard_map/psum | solution.py:48
  55.5 79.2 %all-reduce.11.cloned.1.call-start = ((), (), s32[]{:S(2)}) async-start(), calls=%async_computation.2 | async-start | bytes 262144 | tf_op jit(solution)/shard_map/psum | solution.py:53
  100.5 72.2 %all-reduce.13.cloned.1.call-start = ((), (), s32[]{:S(2)}) async-start(), calls=%async_computation.3 | async-start | bytes 262144 | tf_op jit(solution)/shard_map/psum | solution.py:48
  141.5 67.8 %all-reduce.15.cloned.1.call-start = ((), (), s32[]{:S(2)}) async-start(), calls=%async_computation.4 | async-start | bytes 262144 | tf_op jit(solution)/shard_map/psum | solution.py:48
  172.8 79.1 %all-reduce.17.cloned.1.call-start = ((), (), s32[]{:S(2)}) async-start(), calls=%async_computation.5 | async-start | bytes 262144 | tf_op jit(solution)/shard_map/psum | solution.py:53
  211.9 63.0 %copy-start.6 = (f32[1,256,1024]{2,1,0:T(8,128)S(1)}, f32[1,256,1024]{2,1,0:T(8,128)}, u32[]{:S(2)}) copy-start(f32[1,256,1024]{2,1,0:T(8,128)} %param.16) | copy-start | bytes 3145732
  217.6 129.0 %all-gather.3.cloned.1.call-start = ((), (), s32[]{:S(2)}) async-start(), calls=%async_computation.6 | async-start | bytes 2621440 | tf_op jit(solution)/shard_map/all_gather | solution.py:73
  268.4 6.5 %copy-start.7 = (f32[1,256,1024]{2,1,0:T(8,128)S(1)}, f32[1,256,1024]{2,1,0:T(8,128)}, u32[]{:S(2)}) copy-start(f32[1,256,1024]{2,1,0:T(8,128)} %param.15) | copy-start | bytes 3145732
  272.9 2.0 copy-start.3
  274.9 2.0 copy-start.10
  274.9 20.6 %copy-start.8 = (bf16[128,256]{1,0:T(8,128)(2,1)S(1)}, bf16[128,256]{1,0:T(8,128)(2,1)}, u32[]{:S(2)}) copy-start(bf16[128,256]{1,0:T(8,128)(2,1)} %param.19) | copy-start | bytes 196612
  328.5 13.1 %copy-start.5 = (f32[32,1024]{1,0:T(8,128)S(1)}, f32[32,1024]{1,0:T(8,128)}, u32[]{:S(2)}) copy-start(f32[32,1024]{1,0:T(8,128)} %all-reduce.17.cloned.1.call-done) | copy-start | bytes 393220
  336.8 5.5 %copy-start.2 = (f32[1,1,1024,1024]{3,2,1,0:T(8,128)S(1)}, f32[1,1,1024,1024]{3,2,1,0:T(8,128)}, u32[]{:S(2)}) copy-start(f32[1,1,1024,1024]{3,2,1,0:T(8,128)} %param.12) | copy-start | bytes 12582916
  336.8 6.1 %copy-start.4 = (f32[1024,1024]{1,0:T(8,128)S(1)}, f32[1024,1024]{1,0:T(8,128)}, u32[]{:S(2)}) copy-start(f32[1024,1024]{1,0:T(8,128)} %copy-done.3) | copy-start | bytes 12582916
Sparse Core Ops, SparseCore 0:
  21.4 34.0 all-reduce.6
  57.9 34.4 all-reduce.8
  100.6 34.0 all-reduce.10
  141.7 31.0 all-reduce.12
  174.9 34.4 all-reduce.14
  217.7 34.0 all-reduce.16
  277.0 49.5 all-gather.2
